TPU v7x, 256 devices: a whole 4x4x8 slice. The times are simulated.
256 devices in a mesh: front: 4 (over y_lo, core), blk: 64 (over y_hi, x, z).
Axes of the slice: x: 4, y: 4 (y_hi: 2, y_lo: 2; y = y_hi * 2 + y_lo), z: 8, core: 2. Of those that a mesh axis runs over, the one named last changes fastest.
Arguments:
- front: float32 [4, 8192, 8192], P('front', 'blk'), parts along dimension 0, may hold values from -8 to 40, as said below
- child: float32 [4, 4096, 4096], P('front', 'blk'), parts along dimension 0, may hold values from -1 to 4, as said below
- index_map: int32 [16384], P('front'), parts along dimension 0, may hold values from 0 to 8191, as said below
Outputs:
- factored: float32 [4, 8192, 8192], P('front', 'blk'), parts along dimension 0
There are 4 independent parts, one for each index of `front`. A program takes and returns all parts, laid end to end along the dimension named above; each array names one. Nothing has to cross between parts.
Inputs may be any that keep to these rules, and one draw needn't show every extreme that they name: front is symmetric and positive definite. child is symmetric and positive semidefinite. `index_map`: tile t of the child (indices t * 64 to t * 64 + 63, with t = k * 64 + e and e < 64) maps in increasing order onto 64 different indices of the front's block column b = k * 64 + ((e + h) mod 64), where h is half of 64, that is onto indices b * 128 to b * 128 + 127; no two child indices share a front index.
All inputs are finite; a program needn't handle non-finite values.
Results may differ from a plain program's by a relative error of at most 0.0034.
Values may be sent and summed in bfloat16 or wider, within the bound.
A program may use at most 128 MiB of HBM per device.

v0:
```python
import jax
import jax.numpy as jnp
from jax import lax
from jax.sharding import PartitionSpec as P

PANEL_WIDTH = 512
BLOCK_WIDTH = 128
COL_BLOCKS = 1
TILE_WIDTH = 64
HIGHEST = lax.Precision.HIGHEST


def split_up(shard, dim, count):
    before, after = (shard.shape[:dim], shard.shape[dim + 1 :])
    return jnp.moveaxis(shard.reshape(*before, count, -1, *after), dim, 0)


def sent_and_summed(shard, axis, dim):
    count = lax.axis_size(axis)
    pieces = lax.all_to_all(split_up(shard, dim, count), axis, 0, 0, tiled=True)
    return jnp.sum(pieces, axis=0)


def filled_up(lines, count):
    spare = -lines.shape[0] % count
    if not spare:
        return lines
    return jnp.concatenate([lines, jnp.zeros((spare, *lines.shape[1:]), lines.dtype)])


def from_everyone(shard, axis):
    copies = jnp.broadcast_to(shard, (lax.axis_size(axis), *shard.shape))
    return lax.all_to_all(copies, axis, split_axis=0, concat_axis=0, tiled=True)


def in_order(pieces, dim):
    shape = list(pieces.shape[1:])
    shape[dim] *= pieces.shape[0]
    return jnp.moveaxis(pieces, 0, dim).reshape(shape)


def gathered_copies(shard, axis, dim):
    pieces = from_everyone(shard, axis)
    return in_order(pieces, dim)


def total_of(shard, axes):
    lines = shard.reshape(-1, shard.shape[-1])
    own = sent_and_summed(filled_up(lines, lax.axis_size(axes)), axes, 0)
    whole = gathered_copies(own, axes, 0)
    return whole[: len(lines)].reshape(shard.shape)


def from_behind(shard, axis, by):
    count = lax.axis_size(axis)
    return lax.ppermute(shard, axis, [(i, (i + by) % count) for i in range(count)])


def column_numbers(cycle_size, my_index):
    local_ids = jnp.arange(COL_BLOCKS * BLOCK_WIDTH, dtype=jnp.int32)
    return (
        local_ids // BLOCK_WIDTH * cycle_size + my_index
    ) * BLOCK_WIDTH + local_ids % BLOCK_WIDTH


def row_numbers(cycle_size):
    stored = jnp.arange(cycle_size * COL_BLOCKS * BLOCK_WIDTH, dtype=jnp.int32)
    holder = stored // (COL_BLOCKS * BLOCK_WIDTH)
    within = stored // BLOCK_WIDTH % COL_BLOCKS
    return (within * cycle_size + holder) * BLOCK_WIDTH + stored % BLOCK_WIDTH


def cycle_rows(matrix, cycle_size):
    height = matrix.shape[0]
    return (
        matrix.reshape(height, COL_BLOCKS, cycle_size, BLOCK_WIDTH)
        .transpose(0, 2, 1, 3)
        .reshape(height, -1)
    )


def natural_rows(matrix, cycle_size):
    height = matrix.shape[0]
    return (
        matrix.reshape(height, cycle_size, COL_BLOCKS, BLOCK_WIDTH)
        .transpose(0, 2, 1, 3)
        .reshape(height, -1)
    )


def panel_rows(matrix, row_start, cycle_size):
    first_owner = row_start // BLOCK_WIDTH
    owner_count = PANEL_WIDTH // BLOCK_WIDTH
    height = matrix.shape[0]
    blocks = matrix.reshape(height, cycle_size, COL_BLOCKS, BLOCK_WIDTH)
    return blocks[:, first_owner : first_owner + owner_count, 0, :].reshape(height, PANEL_WIDTH)


def ownership(row_start, my_index):
    first_owner = row_start // BLOCK_WIDTH
    owner_count = PANEL_WIDTH // BLOCK_WIDTH
    is_owner = (my_index >= first_owner) & (my_index < first_owner + owner_count)
    column_start = jnp.clip(my_index - first_owner, 0, owner_count - 1) * BLOCK_WIDTH
    return (is_owner, column_start)


def collect(stacked, row_start, my_index):
    is_owner, column_start = ownership(row_start, my_index)
    padded = jnp.zeros((stacked.shape[0], PANEL_WIDTH, PANEL_WIDTH), jnp.float32)
    padded = lax.dynamic_update_slice(
        padded, jnp.where(is_owner, stacked, 0.0), (0, column_start, 0)
    )
    result = total_of(padded, "blk")
    return result


def own_rows(diag_factor, panel_part, row_start, columns):
    solved = lax.linalg.triangular_solve(
        diag_factor, panel_part, left_side=False, lower=True, transpose_a=True
    )
    offsets = columns - row_start
    diag_rows = jnp.take(diag_factor, jnp.clip(offsets, 0, PANEL_WIDTH - 1), axis=0)
    inside = (offsets >= 0) & (offsets < PANEL_WIDTH)
    before = offsets < 0
    return jnp.where(inside[:, None], diag_rows, jnp.where(before[:, None], 0.0, solved))


def make_refresh(working, lowered, owned_panels, received):
    updated = working - lax.dot_general(
        lowered, received, (((1,), (1,)), ((), ())), preferred_element_type=jnp.float32
    )
    leading = updated
    for is_owner, column_start in owned_panels:
        factor_column = (
            lax.dynamic_slice_in_dim(received, column_start, BLOCK_WIDTH, 1).astype(jnp.float32).T
        )
        leading = jnp.where(is_owner, factor_column, leading)
    return jnp.concatenate([leading, updated[BLOCK_WIDTH:]], axis=0)


def assemble(front, child, index_map, cycle_size, my_index):
    half_cycle = cycle_size // 2
    arrived_tiles = from_behind(child, "blk", half_cycle)
    full_order = 2 * index_map.shape[0]
    tile_places = (index_map % BLOCK_WIDTH).reshape(COL_BLOCKS, cycle_size, TILE_WIDTH)
    places = jnp.arange(BLOCK_WIDTH, dtype=jnp.int32)
    row_table = (tile_places[..., None] == places).astype(jnp.float32)
    shaped = arrived_tiles.reshape(COL_BLOCKS, TILE_WIDTH, COL_BLOCKS, cycle_size, TILE_WIDTH)
    spread = jnp.einsum("acbei,beiq->acbeq", shaped, row_table, precision=HIGHEST)
    spread = jnp.roll(spread, half_cycle, axis=3).reshape(COL_BLOCKS, TILE_WIDTH, full_order)
    source = (my_index - half_cycle) % cycle_size
    own_places = lax.dynamic_index_in_dim(tile_places, source, axis=1, keepdims=False)
    column_table = (own_places[..., None] == places).astype(jnp.float32)
    placed = jnp.einsum("kcq,kcn->kqn", column_table, spread, precision=HIGHEST)
    return front + placed


def on_device(front, child, index_map):
    cycle_size = lax.axis_size("blk")
    my_index = lax.axis_index("blk")
    local_width = COL_BLOCKS * BLOCK_WIDTH
    assembled = assemble(front, child, index_map, cycle_size, my_index).reshape(local_width, -1)
    working = cycle_rows(assembled, cycle_size)
    columns = column_numbers(cycle_size, my_index)
    first_part = panel_rows(working, 0, cycle_size)
    first_diag = collect(first_part[None, :BLOCK_WIDTH], 0, my_index)[0]
    first_rows = own_rows(jnp.linalg.cholesky(first_diag), first_part, 0, columns).astype(
        jnp.bfloat16
    )
    second_part = panel_rows(working, PANEL_WIDTH, cycle_size)
    shared = collect(
        jnp.stack([second_part, first_rows.astype(jnp.float32)]), PANEL_WIDTH, my_index
    )
    crossing = shared[1].astype(jnp.bfloat16)
    second_diag = shared[0] - jnp.dot(crossing, crossing.T, preferred_element_type=jnp.float32)
    second_part = second_part - lax.dot_general(
        first_rows, crossing, (((1,), (1,)), ((), ())), preferred_element_type=jnp.float32
    )
    second_rows = own_rows(
        jnp.linalg.cholesky(second_diag), second_part, PANEL_WIDTH, columns
    ).astype(jnp.bfloat16)
    lowered = jnp.concatenate([first_rows, second_rows], axis=1)
    first_owner = ownership(0, my_index)
    second_owner = ownership(PANEL_WIDTH, my_index)
    owned_panels = (first_owner, (second_owner[0], second_owner[1] + PANEL_WIDTH))
    working = make_refresh(
        working, lowered, owned_panels, lax.all_gather(lowered, "blk", axis=0, tiled=True)
    )
    trailing = columns >= 2 * PANEL_WIDTH
    leading_rows = row_numbers(cycle_size) < 2 * PANEL_WIDTH
    working = jnp.where(trailing[:, None] & leading_rows[None, :], 0.0, working)
    return natural_rows(working, cycle_size).reshape(COL_BLOCKS, BLOCK_WIDTH, -1)


def solution(mesh):
    placed = (P("front", "blk", None), P("front", "blk", None), P("front"))
    return jax.shard_map(
        on_device, mesh=mesh, in_specs=placed, out_specs=P("front", "blk", None), check_vma=False
    )
```

profile of v0, /device:TPU:8, one launch (start us, length us, event | category | flops | bytes accessed | tf_op | source)
XLA Modules:
  0.0 721.6 jit_solution(17179738872541720833)
XLA Ops:
  6.5 2.3 collective-permute-start
  9.7 23.4 %collective-permute-done = f32[1,64,4096]{2,1,0:T(8,128)S(1)} collective-permute-done((f32[1,64,4096]{2,1,0:T(8,128)}, f32[1,64,4096]{2,1,0:T(8,128)S(1)}, u32[]{:S(2)}, u32[]{:S(2)}) %collective-permute-start) | collective-permute-done | bytes 1048608 | tf_op jit(solution)/shard_map/ppermute | solution.py:56
  34.0 3.4 fusion.9
  40.1 3.3 fusion
  45.8 42.7 %all_to_all.20 = f32[64,8,512]{2,1,0:T(8,128)S(1)} all-to-all(f32[64,8,512]{2,1,0:T(8,128)S(1)} %bitcast.161), channel_id=1, replica_groups=mesh['front'=4,'blk'=64] {'blk'}, dimensions={0} | all-to-all | bytes 2097152 | tf_op jit(solution)/shard_map/all_to_all | solution.py:20
  89.7 6.8 all-to-all-start.1
  99.1 25.6 %all-to-all-done.1 = f32[64,8,512]{2,1,0:T(8,128)S(1)} async-done(((f32[64,8,512]{2,1,0:T(8,128)}), f32[64,8,512]{2,1,0:T(8,128)S(1)}, u32[]{:S(2)}, u32[]{:S(2)}) %all-to-all-start.1) | async-done | bytes 1048608 | tf_op jit(solution)/shard_map/all_to_all | solution.py:33
  125.3 11.7 %cholesky.286 = f32[128,128]{1,0:T(8,128)S(1)} custom-call(f32[128,128]{1,0:T(8,128)S(1)} %cholesky.426), custom_call_target="Cholesky" | custom-call | tf_op jit(solution)/shard_map/jit(cholesky)/cholesky | solution.py:167
  137.1 9.8 %custom-call.27 = f32[1,128,128]{1,2,0:T(8,128)S(1)} custom-call(f32[1,128,128]{2,1,0:T(8,128)S(1)} %get-tuple-element.74), custom_call_target="InvertDiagBlocksLowerTriangular" | custom-call | tf_op jit(solution)/shard_map/jit(cholesky)/cholesky | solution.py:167
  147.6 11.7 %cholesky.305 = f32[128,128]{1,0:T(8,128)S(1)} custom-call(f32[128,128]{1,0:T(8,128)S(1)} %cholesky.430), custom_call_target="Cholesky" | custom-call | tf_op jit(solution)/shard_map/jit(cholesky)/cholesky | solution.py:167
  159.4 10.0 %custom-call.28 = f32[1,128,128]{1,2,0:T(8,128)S(1)} custom-call(f32[1,128,128]{2,1,0:T(8,128)S(1)} %get-tuple-element.71), custom_call_target="InvertDiagBlocksLowerTriangular" | custom-call | tf_op jit(solution)/shard_map/jit(cholesky)/cholesky | solution.py:167
  170.0 11.7 %cholesky.326 = f32[128,128]{1,0:T(8,128)S(1)} custom-call(f32[128,128]{1,0:T(8,128)S(1)} %cholesky.435), custom_call_target="Cholesky" | custom-call | tf_op jit(solution)/shard_map/jit(cholesky)/cholesky | solution.py:167
  182.5 9.8 %custom-call.29 = f32[1,128,128]{1,2,0:T(8,128)S(1)} custom-call(f32[1,128,128]{2,1,0:T(8,128)S(1)} %get-tuple-element.68), custom_call_target="InvertDiagBlocksLowerTriangular" | custom-call | tf_op jit(solution)/shard_map/jit(cholesky)/cholesky | solution.py:167
  192.9 11.7 %cholesky.343 = f32[128,128]{1,0:T(8,128)S(1)} custom-call(f32[128,128]{1,0:T(8,128)S(1)} %convolution_subtract_fusion.14), custom_call_target="Cholesky" | custom-call | tf_op jit(solution)/shard_map/jit(cholesky)/cholesky | solution.py:167
  208.9 8.0 %while.4 = (s32[]{:T(128)}, f32[512,512]{1,0:T(8,128)S(1)}, s32[4,2]{0,1:T(2,128)S(1)}, f32[4,128,128]{2,1,0:T(8,128)S(1)}, s32[]{:T(128)}) while((s32[]{:T(128)}, f32[512,512]{1,0:T(8,128)S(1)}, s32[4,2]{0,1:T(2,128)S(1)}, f32[4,128,128]{2,1,0:T(8,128)S(1)}, s32[]{:T(128)}) %tuple.64), condition=%wide.while_cond, body=%wide.while_body.sunk | while | flops 2 | bytes 131181 | solution.py:118
  216.9 39.3 %custom-call.30 = f32[4,128,128]{1,2,0:T(8,128)S(1)} custom-call(f32[4,128,128]{2,1,0:T(8,128)S(1)} %get-tuple-element.22), custom_call_target="InvertDiagBlocksLowerTriangular" | custom-call | tf_op jit(solution)/shard_map/triangular_solve/custom-call.3 | solution.py:118
  260.2 55.7 %all_to_all.21 = f32[64,16,512]{2,1,0:T(8,128)S(1)} all-to-all(f32[64,16,512]{2,1,0:T(8,128)S(1)} %bitcast.158), channel_id=1, replica_groups=mesh['front'=4,'blk'=64] {'blk'}, dimensions={0} | all-to-all | bytes 4194304 | tf_op jit(solution)/shard_map/all_to_all | solution.py:20
  317.7 7.6 %all-to-all-start.3 = ((f32[64,16,512]{2,1,0:T(8,128)}), f32[64,16,512]{2,1,0:T(8,128)S(1)}, u32[]{:S(2)}, u32[]{:S(2)}) async-start(f32[64,16,512]{2,1,0:T(8,128)} %broadcast_in_dim.84), calls=%async_computation.3 | async-start | bytes 4194304 | tf_op jit(solution)/shard_map/all_to_all | solution.py:33
  326.6 47.2 %all-to-all-done.3 = f32[64,16,512]{2,1,0:T(8,128)S(1)} async-done(((f32[64,16,512]{2,1,0:T(8,128)}), f32[64,16,512]{2,1,0:T(8,128)S(1)}, u32[]{:S(2)}, u32[]{:S(2)}) %all-to-all-start.3) | async-done | bytes 2097184 | tf_op jit(solution)/shard_map/all_to_all | solution.py:33
  374.9 2.6 copy.17
  377.5 1.7 convolution_subtract_fusion.1
  380.8 11.7 %cholesky.358 = f32[128,128]{1,0:T(8,128)S(1)} custom-call(f32[128,128]{1,0:T(8,128)S(1)} %cholesky.439), custom_call_target="Cholesky" | custom-call | tf_op jit(solution)/shard_map/jit(cholesky)/cholesky | solution.py:180
  392.7 9.8 %custom-call.31 = f32[1,128,128]{1,2,0:T(8,128)S(1)} custom-call(f32[1,128,128]{2,1,0:T(8,128)S(1)} %get-tuple-element.64), custom_call_target="InvertDiagBlocksLowerTriangular" | custom-call | tf_op jit(solution)/shard_map/jit(cholesky)/cholesky | solution.py:180
  405.0 11.7 %cholesky.377 = f32[128,128]{1,0:T(8,128)S(1)} custom-call(f32[128,128]{1,0:T(8,128)S(1)} %cholesky.443), custom_call_target="Cholesky" | custom-call | tf_op jit(solution)/shard_map/jit(cholesky)/cholesky | solution.py:180
  418.1 9.9 %custom-call.32 = f32[1,128,128]{1,2,0:T(8,128)S(1)} custom-call(f32[1,128,128]{2,1,0:T(8,128)S(1)} %get-tuple-element.61), custom_call_target="InvertDiagBlocksLowerTriangular" | custom-call | tf_op jit(solution)/shard_map/jit(cholesky)/cholesky | solution.py:180
  429.6 11.7 %cholesky.398 = f32[128,128]{1,0:T(8,128)S(1)} custom-call(f32[128,128]{1,0:T(8,128)S(1)} %cholesky.448), custom_call_target="Cholesky" | custom-call | tf_op jit(solution)/shard_map/jit(cholesky)/cholesky | solution.py:180
  442.0 9.8 %custom-call.33 = f32[1,128,128]{1,2,0:T(8,128)S(1)} custom-call(f32[1,128,128]{2,1,0:T(8,128)S(1)} %get-tuple-element.58), custom_call_target="InvertDiagBlocksLowerTriangular" | custom-call | tf_op jit(solution)/shard_map/jit(cholesky)/cholesky | solution.py:180
  453.3 11.9 %cholesky.415 = f32[128,128]{1,0:T(8,128)S(1)} custom-call(f32[128,128]{1,0:T(8,128)S(1)} %convolution_subtract_fusion.12), custom_call_target="Cholesky" | custom-call | tf_op jit(solution)/shard_map/jit(cholesky)/cholesky | solution.py:180
  468.7 8.1 %while.5 = (s32[]{:T(128)}, f32[512,512]{1,0:T(8,128)S(1)}, s32[4,2]{0,1:T(2,128)S(1)}, f32[4,128,128]{2,1,0:T(8,128)S(1)}, s32[]{:T(128)}) while((s32[]{:T(128)}, f32[512,512]{1,0:T(8,128)S(1)}, s32[4,2]{0,1:T(2,128)S(1)}, f32[4,128,128]{2,1,0:T(8,128)S(1)}, s32[]{:T(128)}) %tuple.72), condition=%wide.while_cond.clone, body=%wide.while_body.clone.sunk | while | flops 2 | bytes 131181 | solution.py:118
  476.8 39.3 %custom-call.34 = f32[4,128,128]{1,2,0:T(8,128)S(1)} custom-call(f32[4,128,128]{2,1,0:T(8,128)S(1)} %get-tuple-element.23), custom_call_target="InvertDiagBlocksLowerTriangular" | custom-call | tf_op jit(solution)/shard_map/triangular_solve/custom-call.3 | solution.py:118
  520.7 180.0 %all-gather.2.cloned.1.call-done = bf16[8192,1024]{0,1:T(8,128)(2,1)} async-done(((bf16[128,1024]{0,1:T(8,128)(2,1)}), bf16[8192,1024]{0,1:T(8,128)(2,1)}) %all-gather.2.cloned.1.call-update) | async-done | bytes 16777232 | tf_op jit(solution)/shard_map/all_gather | solution.py:187
  700.7 13.8 %fusion.4 = f32[1,128,8192]{2,1,0:T(8,128)} fusion(bf16[8192,1024]{0,1:T(8,128)(2,1)} %all-gather.2.cloned.1.call-done, f32[1,128,8192]{2,1,0:T(8,128)} %copy-done, s32[]{:T(128)S(6)} %select_n.184, s32[]{:T(128)S(6)} %select_n.182, pred[]{:T(512)S(6)} %and.158, pred[]{:T(512)S(6)} %and.156, pred[8192]{0:T(1024)(128)(4,1)S(1)} %fusion.83, ...), kind=kOutput, calls=%fused_computation.12 | convolution fusion | flops 2155347968 | bytes 29630602 | tf_op jit(solution)/shard_map/dot_general | solution.py:129
  (145 shorter events, 54.3 us)
Async XLA Ops:
  6.5 26.6 %collective-permute-start = (f32[1,64,4096]{2,1,0:T(8,128)}, f32[1,64,4096]{2,1,0:T(8,128)S(1)}, u32[]{:S(2)}, u32[]{:S(2)}) collective-permute-start(f32[1,64,4096]{2,1,0:T(8,128)} %param.9), channel_id=1, source_target_pairs={{0,32},{1,33},{2,34},{3,35},{4,36},{5,37},{6,38},{7,39},{8,40},{9,... | collective-permute-start | bytes 3145736 | tf_op jit(solution)/shard_map/ppermute | solution.py:56
  37.9 2.2 copy-start.1
  43.4 2.0 copy-start
  89.7 35.0 %all-to-all-start.1 = ((f32[64,8,512]{2,1,0:T(8,128)}), f32[64,8,512]{2,1,0:T(8,128)S(1)}, u32[]{:S(2)}, u32[]{:S(2)}) async-start(f32[64,8,512]{2,1,0:T(8,128)} %broadcast_in_dim.78), calls=%async_computation.1 | async-start | bytes 2097152 | tf_op jit(solution)/shard_map/all_to_all | solution.py:33
  192.9 63.4 %copy-start.3 = (f32[16,8,4,128]{3,1,2,0:T(8,128)S(1)}, f32[16,8,4,128]{3,1,2,0:T(8,128)}, u32[]{:S(2)}) copy-start(f32[16,8,4,128]{3,1,2,0:T(8,128)} %copy.37) | copy-start | bytes 786436
  208.9 50.7 %copy-start.6 = (pred[128]{0:T(512)(128)(4,1)S(1)}, pred[128]{0:T(512)(128)(4,1)}, u32[]{:S(2)}) copy-start(pred[128]{0:T(512)(128)(4,1)} %get-tuple-element.84) | copy-start | bytes 388
  208.9 50.7 %copy-start.7 = (pred[128]{0:T(512)(128)(4,1)S(1)}, pred[128]{0:T(512)(128)(4,1)}, u32[]{:S(2)}) copy-start(pred[128]{0:T(512)(128)(4,1)} %get-tuple-element.86) | copy-start | bytes 388
  317.7 8.1 %copy-start.8 = (s32[128]{0:T(128)S(1)}, s32[128]{0:T(128)}, u32[]{:S(2)}) copy-start(s32[128]{0:T(128)} %get-tuple-element.79) | copy-start | bytes 1540
  317.7 56.1 %all-to-all-start.3 = ((f32[64,16,512]{2,1,0:T(8,128)}), f32[64,16,512]{2,1,0:T(8,128)S(1)}, u32[]{:S(2)}, u32[]{:S(2)}) async-start(f32[64,16,512]{2,1,0:T(8,128)} %broadcast_in_dim.84), calls=%async_computation.3 | async-start | bytes 4194304 | tf_op jit(solution)/shard_map/all_to_all | solution.py:33
  325.3 375.4 %all-gather.2.cloned.1.call-start = ((), (), s32[]{:S(2)}) async-start(), calls=%async_computation.4 | async-start | bytes 17039360 | tf_op jit(solution)/shard_map/all_gather | solution.py:187
  379.8 1.0 copy-start.2
  452.1 64.1 %copy-start.4 = (f32[128,512]{1,0:T(8,128)S(1)}, f32[128,512]{1,0:T(8,128)}, u32[]{:S(2)}) copy-start(f32[128,512]{1,0:T(8,128)} %copy.23) | copy-start | bytes 786436
  516.2 3.7 copy-start.5
Sparse Core Ops, SparseCore 0:
  520.8 179.8 all-gather.1
where the time goes:
time: 730 us; the launch traced here: 722 us
  waiting for transfers between devices  276 us (38%)
  other arithmetic  241 us (33%)
  blocking collectives  98.4 us (13%)
  matrix products  34.4 us (5%)
  local copies, waits for them, and re-layouts  34.3 us (5%)
  between operations  19.4 us (3%)
  starting transfers between devices  17.2 us (2%)
    all_gather x1, waiting for transfers between devices, on_device(): lax.all_gather(lowered, 'blk', axis=0, tiled=True)  180 us
    all_to_all x2, blocking collectives, sent_and_summed(): pieces = lax.all_to_all(split_up(shard, dim, count), axis, 0, 0, tiled=True)  98.4 us
    another operation x15, other arithmetic, on_device(): jnp.linalg.cholesky(second_diag)  79.4 us
    another operation x5, other arithmetic, own_rows(): lax.linalg.triangular_solve(diag_factor, panel_part, left_side=False, low...  79 us
    another operation x14, other arithmetic, on_device(): jnp.linalg.cholesky(first_diag)  78.8 us
    all_to_all x2, waiting for transfers between devices, from_everyone(): return lax.all_to_all(copies, axis, split_axis=0, concat_axis=0, tiled=True)  72.8 us
    ppermute x1, waiting for transfers between devices, from_behind(): lax.ppermute(shard, axis, [(i, (i + by) % count) for i in range(count)])  23.4 us
    another operation x27, local copies, waits for them, and re-layouts, own_rows(): lax.linalg.triangular_solve(diag_factor, panel_part, left_side=False, low...  16 us
  transfers between devices with their start and end apart: 4, of which 4 were waited for; matrix products, arithmetic and copies ran while one was open for 1% of the time, Pallas kernels for 0%

commit v1 on v0

--- a/solution.py
+++ b/solution.py
@@ -184,7 +184,12 @@
     second_owner = ownership(PANEL_WIDTH, my_index)
     owned_panels = (first_owner, (second_owner[0], second_owner[1] + PANEL_WIDTH))
     working = make_refresh(
-        working, lowered, owned_panels, lax.all_gather(lowered, "blk", axis=0, tiled=True)
+        working,
+        lowered,
+        owned_panels,
+        jnp.concatenate(
+            lax.all_to_all(jnp.stack([lowered] * lax.axis_size("blk")), "blk", 0, 0), axis=0
+        ),
     )
     trailing = columns >= 2 * PANEL_WIDTH
     leading_rows = row_numbers(cycle_size) < 2 * PANEL_WIDTH

time: 730 us -> 922 us (1.26)
  the two profiles are of different devices: /device:TPU:8 before, /device:TPU:36 now
where the time goes in v1:
time: 922 us; the launch traced here: 914 us
  waiting for transfers between devices  466 us (51%)
  other arithmetic  241 us (26%)
  blocking collectives  99.3 us (11%)
  local copies, waits for them, and re-layouts  49.3 us (5%)
  matrix products  26.8 us (3%)
  starting transfers between devices  25.5 us (3%)
    all_to_all x1, waiting for transfers between devices, on_device(): lax.all_to_all(jnp.stack([lowered] * lax.axis_size('blk')), 'blk', 0, 0)  371 us
    all_to_all x2, blocking collectives, sent_and_summed(): pieces = lax.all_to_all(split_up(shard, dim, count), axis, 0, 0, tiled=True)  99.3 us
    another operation x15, other arithmetic, on_device(): jnp.linalg.cholesky(second_diag)  79.4 us
    another operation x5, other arithmetic, own_rows(): lax.linalg.triangular_solve(diag_factor, panel_part, left_side=False, low...  79 us
    another operation x14, other arithmetic, on_device(): jnp.linalg.cholesky(first_diag)  78.8 us
    all_to_all x2, waiting for transfers between devices, from_everyone(): return lax.all_to_all(copies, axis, split_axis=0, concat_axis=0, tiled=True)  72.5 us
    ppermute x1, waiting for transfers between devices, from_behind(): lax.ppermute(shard, axis, [(i, (i + by) % count) for i in range(count)])  22.5 us
  transfers between devices with their start and end apart: 4, of which 4 were waited for; matrix products, arithmetic and copies ran while one was open for 0% of the time, Pallas kernels for 0%

profile of v1, /device:TPU:36, one launch (start us, length us, event | category | flops | bytes accessed | tf_op | source)
XLA Modules:
  0.0 913.6 jit_solution(9900221301815594237)
XLA Ops:
  4.1 22.5 %collective-permute-done = f32[1,64,4096]{2,1,0:T(8,128)S(1)} collective-permute-done((f32[1,64,4096]{2,1,0:T(8,128)}, f32[1,64,4096]{2,1,0:T(8,128)S(1)}, u32[]{:S(2)}, u32[]{:S(2)}) %collective-permute-start) | collective-permute-done | bytes 1048608 | tf_op jit(solution)/shard_map/ppermute | solution.py:56
  27.5 3.4 fusion.9
  33.5 3.4 fusion
  39.4 42.6 %all_to_all.25 = f32[64,8,512]{2,1,0:T(8,128)S(1)} all-to-all(f32[64,8,512]{2,1,0:T(8,128)S(1)} %bitcast.170), channel_id=1, replica_groups=mesh['front'=4,'blk'=64] {'blk'}, dimensions={0} | all-to-all | bytes 2097152 | tf_op jit(solution)/shard_map/all_to_all | solution.py:20
  83.1 7.5 all-to-all-start.1
  94.0 24.0 %all-to-all-done.1 = f32[64,8,512]{2,1,0:T(8,128)S(1)} async-done(((f32[64,8,512]{2,1,0:T(8,128)}), f32[64,8,512]{2,1,0:T(8,128)S(1)}, u32[]{:S(2)}, u32[]{:S(2)}) %all-to-all-start.1) | async-done | bytes 1048608 | tf_op jit(solution)/shard_map/all_to_all | solution.py:33
  118.6 11.7 %cholesky.286 = f32[128,128]{1,0:T(8,128)S(1)} custom-call(f32[128,128]{1,0:T(8,128)S(1)} %cholesky.426), custom_call_target="Cholesky" | custom-call | tf_op jit(solution)/shard_map/jit(cholesky)/cholesky | solution.py:167
  130.5 9.8 %custom-call.27 = f32[1,128,128]{1,2,0:T(8,128)S(1)} custom-call(f32[1,128,128]{2,1,0:T(8,128)S(1)} %get-tuple-element.74), custom_call_target="InvertDiagBlocksLowerTriangular" | custom-call | tf_op jit(solution)/shard_map/jit(cholesky)/cholesky | solution.py:167
  141.0 11.7 %cholesky.305 = f32[128,128]{1,0:T(8,128)S(1)} custom-call(f32[128,128]{1,0:T(8,128)S(1)} %cholesky.430), custom_call_target="Cholesky" | custom-call | tf_op jit(solution)/shard_map/jit(cholesky)/cholesky | solution.py:167
  152.7 9.9 %custom-call.28 = f32[1,128,128]{1,2,0:T(8,128)S(1)} custom-call(f32[1,128,128]{2,1,0:T(8,128)S(1)} %get-tuple-element.71), custom_call_target="InvertDiagBlocksLowerTriangular" | custom-call | tf_op jit(solution)/shard_map/jit(cholesky)/cholesky | solution.py:167
  163.4 11.7 %cholesky.326 = f32[128,128]{1,0:T(8,128)S(1)} custom-call(f32[128,128]{1,0:T(8,128)S(1)} %cholesky.435), custom_call_target="Cholesky" | custom-call | tf_op jit(solution)/shard_map/jit(cholesky)/cholesky | solution.py:167
  175.8 9.8 %custom-call.29 = f32[1,128,128]{1,2,0:T(8,128)S(1)} custom-call(f32[1,128,128]{2,1,0:T(8,128)S(1)} %get-tuple-element.68), custom_call_target="InvertDiagBlocksLowerTriangular" | custom-call | tf_op jit(solution)/shard_map/jit(cholesky)/cholesky | solution.py:167
  186.2 11.7 %cholesky.343 = f32[128,128]{1,0:T(8,128)S(1)} custom-call(f32[128,128]{1,0:T(8,128)S(1)} %convolution_subtract_fusion.14), custom_call_target="Cholesky" | custom-call | tf_op jit(solution)/shard_map/jit(cholesky)/cholesky | solution.py:167
  202.2 7.8 while.4
  210.0 39.3 %custom-call.30 = f32[4,128,128]{1,2,0:T(8,128)S(1)} custom-call(f32[4,128,128]{2,1,0:T(8,128)S(1)} %get-tuple-element.22), custom_call_target="InvertDiagBlocksLowerTriangular" | custom-call | tf_op jit(solution)/shard_map/triangular_solve/custom-call.3 | solution.py:118
  253.4 56.7 %all_to_all.26 = f32[64,16,512]{2,1,0:T(8,128)S(1)} all-to-all(f32[64,16,512]{2,1,0:T(8,128)S(1)} %bitcast.167), channel_id=1, replica_groups=mesh['front'=4,'blk'=64] {'blk'}, dimensions={0} | all-to-all | bytes 4194304 | tf_op jit(solution)/shard_map/all_to_all | solution.py:20
  311.8 7.6 all-to-all-start.3
  319.4 48.5 %all-to-all-done.3 = f32[64,16,512]{2,1,0:T(8,128)S(1)} async-done(((f32[64,16,512]{2,1,0:T(8,128)}), f32[64,16,512]{2,1,0:T(8,128)S(1)}, u32[]{:S(2)}, u32[]{:S(2)}) %all-to-all-start.3) | async-done | bytes 2097184 | tf_op jit(solution)/shard_map/all_to_all | solution.py:33
  374.9 11.7 %cholesky.358 = f32[128,128]{1,0:T(8,128)S(1)} custom-call(f32[128,128]{1,0:T(8,128)S(1)} %cholesky.439), custom_call_target="Cholesky" | custom-call | tf_op jit(solution)/shard_map/jit(cholesky)/cholesky | solution.py:180
  386.8 9.8 %custom-call.31 = f32[1,128,128]{1,2,0:T(8,128)S(1)} custom-call(f32[1,128,128]{2,1,0:T(8,128)S(1)} %get-tuple-element.64), custom_call_target="InvertDiagBlocksLowerTriangular" | custom-call | tf_op jit(solution)/shard_map/jit(cholesky)/cholesky | solution.py:180
  399.1 11.7 %cholesky.377 = f32[128,128]{1,0:T(8,128)S(1)} custom-call(f32[128,128]{1,0:T(8,128)S(1)} %cholesky.443), custom_call_target="Cholesky" | custom-call | tf_op jit(solution)/shard_map/jit(cholesky)/cholesky | solution.py:180
  412.3 9.9 %custom-call.32 = f32[1,128,128]{1,2,0:T(8,128)S(1)} custom-call(f32[1,128,128]{2,1,0:T(8,128)S(1)} %get-tuple-element.61), custom_call_target="InvertDiagBlocksLowerTriangular" | custom-call | tf_op jit(solution)/shard_map/jit(cholesky)/cholesky | solution.py:180
  423.8 11.7 %cholesky.398 = f32[128,128]{1,0:T(8,128)S(1)} custom-call(f32[128,128]{1,0:T(8,128)S(1)} %cholesky.448), custom_call_target="Cholesky" | custom-call | tf_op jit(solution)/shard_map/jit(cholesky)/cholesky | solution.py:180
  436.2 9.8 %custom-call.33 = f32[1,128,128]{1,2,0:T(8,128)S(1)} custom-call(f32[1,128,128]{2,1,0:T(8,128)S(1)} %get-tuple-element.58), custom_call_target="InvertDiagBlocksLowerTriangular" | custom-call | tf_op jit(solution)/shard_map/jit(cholesky)/cholesky | solution.py:180
  447.4 11.9 %cholesky.415 = f32[128,128]{1,0:T(8,128)S(1)} custom-call(f32[128,128]{1,0:T(8,128)S(1)} %convolution_subtract_fusion.12), custom_call_target="Cholesky" | custom-call | tf_op jit(solution)/shard_map/jit(cholesky)/cholesky | solution.py:180
  462.7 8.3 while.5
  471.1 39.3 %custom-call.34 = f32[4,128,128]{1,2,0:T(8,128)S(1)} custom-call(f32[4,128,128]{2,1,0:T(8,128)S(1)} %get-tuple-element.23), custom_call_target="InvertDiagBlocksLowerTriangular" | custom-call | tf_op jit(solution)/shard_map/triangular_solve/custom-call.3 | solution.py:118
  514.1 6.2 stack.12
  520.4 7.2 all-to-all-start.4
  527.6 370.7 %all-to-all-done.4 = bf16[64,128,1024]{1,2,0:T(8,128)(2,1)} async-done(((bf16[64,128,1024]{1,2,0:T(8,128)(2,1)}), bf16[64,128,1024]{1,2,0:T(8,128)(2,1)}, u32[]{:S(2)}, u32[]{:S(2)}) %all-to-all-start.4) | async-done | bytes 16777248 | tf_op jit(solution)/shard_map/all_to_all | solution.py:191
  898.4 9.0 copy_bitcast_fusion
  907.4 6.0 fusion.4
  (147 shorter events, 60.5 us)
Async XLA Ops:
  0.0 26.6 %collective-permute-start = (f32[1,64,4096]{2,1,0:T(8,128)}, f32[1,64,4096]{2,1,0:T(8,128)S(1)}, u32[]{:S(2)}, u32[]{:S(2)}) collective-permute-start(f32[1,64,4096]{2,1,0:T(8,128)} %param.9), channel_id=1, source_target_pairs={{0,32},{1,33},{2,34},{3,35},{4,36},{5,37},{6,38},{7,39},{8,40},{9,... | collective-permute-start | bytes 3145736 | tf_op jit(solution)/shard_map/ppermute | solution.py:56
  31.3 2.2 copy-start.2
  37.0 2.0 copy-start
  83.1 34.9 %all-to-all-start.1 = ((f32[64,8,512]{2,1,0:T(8,128)}), f32[64,8,512]{2,1,0:T(8,128)S(1)}, u32[]{:S(2)}, u32[]{:S(2)}) async-start(f32[64,8,512]{2,1,0:T(8,128)} %broadcast_in_dim.78), calls=%async_computation.1 | async-start | bytes 2097152 | tf_op jit(solution)/shard_map/all_to_all | solution.py:33
  186.2 63.1 %copy-start.5 = (f32[16,8,4,128]{3,1,2,0:T(8,128)S(1)}, f32[16,8,4,128]{3,1,2,0:T(8,128)}, u32[]{:S(2)}) copy-start(f32[16,8,4,128]{3,1,2,0:T(8,128)} %copy.48) | copy-start | bytes 786436
  202.2 50.5 %copy-start.7 = (pred[128]{0:T(512)(128)(4,1)S(1)}, pred[128]{0:T(512)(128)(4,1)}, u32[]{:S(2)}) copy-start(pred[128]{0:T(512)(128)(4,1)} %get-tuple-element.84) | copy-start | bytes 388
  202.2 50.5 %copy-start.8 = (pred[128]{0:T(512)(128)(4,1)S(1)}, pred[128]{0:T(512)(128)(4,1)}, u32[]{:S(2)}) copy-start(pred[128]{0:T(512)(128)(4,1)} %get-tuple-element.86) | copy-start | bytes 388
  210.0 42.8 %copy-start.4 = (f32[128,4,1,128]{0,3,1,2:T(8,128)S(1)}, f32[128,4,1,128]{0,3,1,2:T(8,128)}, u32[]{:S(2)}) copy-start(f32[128,4,1,128]{0,3,1,2:T(8,128)} %copy.24) | copy-start | bytes 786436
  311.8 7.6 copy-start.9
  311.8 56.1 %all-to-all-start.3 = ((f32[64,16,512]{2,1,0:T(8,128)}), f32[64,16,512]{2,1,0:T(8,128)S(1)}, u32[]{:S(2)}, u32[]{:S(2)}) async-start(f32[64,16,512]{2,1,0:T(8,128)} %broadcast_in_dim.84), calls=%async_computation.3 | async-start | bytes 4194304 | tf_op jit(solution)/shard_map/all_to_all | solution.py:33
  373.9 1.0 copy-start.3
  510.4 3.7 copy-start.6
  520.4 378.0 %all-to-all-start.4 = ((bf16[64,128,1024]{1,2,0:T(8,128)(2,1)}), bf16[64,128,1024]{1,2,0:T(8,128)(2,1)}, u32[]{:S(2)}, u32[]{:S(2)}) async-start(bf16[64,128,1024]{1,2,0:T(8,128)(2,1)} %stack.12), calls=%async_computation.4 | async-start | bytes 33554432 | tf_op jit(solution)/shard_map/all_to_all | solution.py:191
  898.4 9.0 copy-start.1
